TPU v7x, 512 devices: a whole 4x4x16 slice. The times are simulated.
512 devices in a mesh: req: 128 (over y, z, core), tp: 4 (over x).
Axes of the slice: x: 4, y: 4, z: 16, core: 2. Of those that a mesh axis runs over, the one named last changes fastest.
Arguments:
- queries: bfloat16 [32768, 2048], P('req', 'tp'), may hold values from -160 to 160
- key_rows: bfloat16 [32768, 2048], P('req', 'tp'), may hold values from -6 to 6
- value_rows: bfloat16 [32768, 2048], P('req', 'tp'), may hold values from -6 to 6
- lengths: int32 [128, 4], P('req'), may hold values from 1 to 128, 256 in all within a row
- adapter_ids: int32 [128, 4], P('req'), may hold values from 0 to 127, as said below
- adapter_home: int32 [128], replicated, may hold values from 0 to 127, each once
- adapter_down: bfloat16 [128, 2048, 16], P('req', 'tp'), may hold values from -0.125 to 0.125
- adapter_up: bfloat16 [128, 16, 2048], P('req'), may hold values from -4 to 4
- output_weight: bfloat16 [2048, 2048], P('tp'), may hold values from -0.125 to 0.125
Outputs:
- block_output: bfloat16 [32768, 2048], P('req', 'tp')
Inputs may be any that keep to these rules, and one draw needn't show every extreme that they name: `adapter_ids`: all prompts together name exactly 16 distinct adapters.
All inputs are finite; a program needn't handle non-finite values.
Results may differ from a plain program's by a relative error of at most 0.0055.
Values may be sent and summed in bfloat16 or wider, within the bound.
A program may use at most 64 MiB of HBM per device.

v0:
```python
import math
import jax
import jax.numpy as jnp
from jax import lax
from jax.sharding import PartitionSpec as P

HD = 128


def segment_rows(length_row, row_total):
    boundary = jnp.cumsum(length_row)
    position = jnp.arange(row_total, dtype=jnp.int32)
    return jnp.sum((position[:, None] >= boundary[None, :]).astype(jnp.int32), axis=1)


def attend(queries, key_rows, value_rows, segment):
    row_total = queries.shape[0]
    head_count = queries.shape[1] // HD
    shaped_q = queries.reshape(row_total, head_count, HD)
    shaped_k = key_rows.reshape(row_total, head_count, HD)
    shaped_v = value_rows.reshape(row_total, head_count, HD)
    scores = jnp.einsum("qhd,khd->hqk", shaped_q, shaped_k, preferred_element_type=jnp.float32) * (
        1.0 / math.sqrt(HD)
    )
    position = jnp.arange(row_total, dtype=jnp.int32)
    allowed = (segment[:, None] == segment[None, :]) & (position[None, :] <= position[:, None])
    masked = jnp.where(allowed[None], scores, -1e30)
    highest = jnp.max(masked, axis=2, keepdims=True)
    exponent = jnp.where(allowed[None], jnp.exp(masked - highest), 0.0)
    weights = (exponent / jnp.sum(exponent, axis=2, keepdims=True)).astype(jnp.bfloat16)
    mixed = jnp.einsum("hqk,khd->qhd", weights, shaped_v, preferred_element_type=jnp.float32)
    return mixed.reshape(row_total, head_count * HD).astype(jnp.bfloat16)


def lowrank_delta(rank_rows, onehot, factor_up):
    row_total, prompts = onehot.shape
    rank_size = rank_rows.shape[1]
    spread = (onehot[:, :, None] * rank_rows[:, None, :]).reshape(row_total, prompts * rank_size)
    upper = factor_up.astype(jnp.float32).reshape(prompts * rank_size, factor_up.shape[2])
    return jnp.dot(spread, upper, precision=lax.Precision.HIGHEST)


def body(
    queries,
    key_rows,
    value_rows,
    lengths,
    adapter_ids,
    adapter_home,
    adapter_down,
    adapter_up,
    output_weight,
):
    row_total = queries.shape[0]
    prompts = lengths.shape[1]
    segment = segment_rows(lengths[0], row_total)
    prompt_ids = adapter_ids[0]
    downs_all, uppers_all = (
        lax.all_gather(adapter_down, "req", axis=0, tiled=True),
        lax.all_gather(adapter_up, "req", axis=0, tiled=True),
    )
    slot_rows = adapter_home[prompt_ids]
    downs = downs_all[slot_rows]
    uppers = uppers_all[slot_rows]
    attended = attend(queries, key_rows, value_rows, segment)
    onehot = (segment[:, None] == jnp.arange(prompts, dtype=jnp.int32)[None, :]).astype(jnp.float32)
    per_prompt = jnp.einsum("ta,sar->str", attended, downs, preferred_element_type=jnp.float32)
    low_local = jnp.einsum("ts,str->tr", onehot, per_prompt, precision=lax.Precision.HIGHEST)
    base_rows = jnp.dot(attended, output_weight, preferred_element_type=jnp.float32)
    partial_rows = base_rows + lowrank_delta(low_local, onehot, uppers)
    summed = lax.psum_scatter(partial_rows, "tp", scatter_dimension=1, tiled=True)
    return summed.astype(jnp.bfloat16)


def solution(mesh):
    return jax.shard_map(
        body,
        mesh=mesh,
        in_specs=(
            P("req", "tp"),
            P("req", "tp"),
            P("req", "tp"),
            P("req", None),
            P("req", None),
            P(),
            P("req", "tp", None),
            P("req", None, None),
            P("tp", None),
        ),
        out_specs=P("req", "tp"),
        check_vma=False,
    )
```

profile of v0, /device:TPU:1, one launch (start us, length us, event | category | flops | bytes accessed | tf_op | source)
XLA Modules:
  0.0 350.7 jit_solution(13716006195187594143)
XLA Ops:
  6.5 0.7 all-gather.3.cloned.1.call-update
  7.3 0.0 all-gather.5.cloned.1.call-start
  7.3 0.7 all-gather.5.cloned.1.call-update
  8.0 0.0 copy-start.1
  8.0 0.0 reduce-scatter.2.cloned.1.call-start
  8.1 1.8 copy.35
  9.9 0.7 fusion.20
  10.6 1.3 gather_fusion
  11.8 0.8 reduce-window.8
  12.7 0.1 convert_reduce_fusion
  12.8 0.1 fusion.11
  12.9 1.6 fusion.26
  14.5 1.3 fusion.4
  15.8 1.4 convolution_convert_fusion
  17.2 139.8 %all-gather.3.cloned.1.call-done = bf16[128,512,16]{1,2,0:T(8,128)(2,1)} async-done(((bf16[1,512,16]{1,2,0:T(8,128)(2,1)}), bf16[128,512,16]{1,2,0:T(8,128)(2,1)}) %all-gather.3.cloned.1.call-update) | async-done | bytes 2097168 | tf_op jit(solution)/shard_map/all_gather | solution.py:59
  157.0 2.1 gather_fusion.1
  159.1 0.2 fusion.6
  159.3 144.2 %all-gather.5.cloned.1.call-done = bf16[128,16,2048]{2,1,0:T(8,128)(2,1)} async-done(((bf16[1,16,2048]{2,1,0:T(8,128)(2,1)}), bf16[128,16,2048]{2,1,0:T(8,128)(2,1)}) %all-gather.5.cloned.1.call-update) | async-done | bytes 8388624 | tf_op jit(solution)/shard_map/all_gather | solution.py:60
  303.5 3.9 %gather_fusion.2 = bf16[4,16,2048]{2,1,0:T(8,128)(2,1)S(1)} fusion(bf16[128,16,2048]{2,1,0:T(8,128)(2,1)} %all-gather.5.cloned.1.call-done, s32[1024]{0:T(1024)S(1)} %pad_clamp_fusion), kind=kCustom, calls=%fused_computation.2 | custom fusion | bytes 524304 | tf_op jit(solution)/shard_map/gather | solution.py:64
  307.5 1.0 convolution_bitcast_fusion
  308.5 2.1 convolution_add_fusion
  310.6 0.0 reduce-scatter.2.cloned.1.call-update
  310.6 31.8 %reduce-scatter.2.cloned.1.call-done = f32[256,512]{1,0:T(8,128)} async-done(((f32[256,2048]{1,0:T(8,128)}), f32[256,512]{1,0:T(8,128)}) %reduce-scatter.2.cloned.1.call-update) | async-done | bytes 524304 | tf_op jit(solution)/shard_map/reduce_scatter | solution.py:71
  342.4 1.8 convert_element_type.32
  (8 shorter events, 0.0 us)
Async XLA Ops:
  6.5 302.0 %copy-start = (bf16[512,2048]{1,0:T(8,128)(2,1)S(1)}, bf16[512,2048]{1,0:T(8,128)(2,1)}, u32[]{:S(2)}) copy-start(bf16[512,2048]{1,0:T(8,128)(2,1)} %param.17) | copy-start | bytes 6291460
  6.5 150.4 %all-gather.3.cloned.1.call-start = ((), (), s32[]{:S(2)}) async-start(), calls=%async_computation.1 | async-start | bytes 2113536 | tf_op jit(solution)/shard_map/all_gather | solution.py:59
  7.3 296.3 %all-gather.5.cloned.1.call-start = ((), (), s32[]{:S(2)}) async-start(), calls=%async_computation.2 | async-start | bytes 8454144 | tf_op jit(solution)/shard_map/all_gather | solution.py:60
  8.0 6.5 %copy-start.1 = (bf16[256,512]{1,0:T(8,128)(2,1)S(1)}, bf16[256,512]{1,0:T(8,128)(2,1)}, u32[]{:S(2)}) copy-start(bf16[256,512]{1,0:T(8,128)(2,1)} %param.10) | copy-start | bytes 786436
  8.0 334.4 %reduce-scatter.2.cloned.1.call-start = ((), (), s32[]{:S(2)}) async-start(), calls=%async_computation.3 | async-start | bytes 2621440 | tf_op jit(solution)/shard_map/reduce_scatter | solution.py:71
Sparse Core Ops, SparseCore 0:
  10.5 146.4 all-gather.2
  160.1 143.3 all-gather.4
  310.8 31.6 reduce-scatter.1
where the time goes:
time: 351 us
  waiting for transfers between devices  317 us (90%)
  between operations  13.2 us (4%)
  local copies, waits for them, and re-layouts  9.21 us (3%)
  matrix products  7.58 us (2%)
    all_gather x1, waiting for transfers between devices, body(): lax.all_gather(adapter_up, 'req', axis=0, tiled=True)  144 us
    all_gather x1, waiting for transfers between devices, body(): lax.all_gather(adapter_down, 'req', axis=0, tiled=True)  140 us
    reduce_scatter x1, waiting for transfers between devices, body(): lax.psum_scatter(partial_rows, 'tp', scatter_dimension=1, tiled=True)  31.8 us
  transfers between devices with their start and end apart: 3, of which 3 were waited for; matrix products, arithmetic and copies ran while one was open for 3% of the time, Pallas kernels for 0%

commit v1 on v0

--- a/solution.py
+++ b/solution.py
@@ -56,7 +56,9 @@
     segment = segment_rows(lengths[0], row_total)
     prompt_ids = adapter_ids[0]
     downs_all, uppers_all = (
-        lax.all_gather(adapter_down, "req", axis=0, tiled=True),
+        jnp.concatenate(
+            lax.all_to_all(jnp.stack([adapter_down] * lax.axis_size("req")), "req", 0, 0), axis=0
+        ),
         lax.all_gather(adapter_up, "req", axis=0, tiled=True),
     )
     slot_rows = adapter_home[prompt_ids]

time: 351 us -> 227 us (0.65)
  waiting for transfers between devices: 317 us -> 173 us
  starting transfers between devices: 0.08 us -> 21.2 us
    all_gather x1 -> x0, waiting for transfers between devices: 140 us -> none  [body(): lax.all_gather(adapter_down, 'req', axis=0, tiled=True)]
    all_gather x1, waiting for transfers between devices: 144 us -> 36.4 us  [body(): lax.all_gather(adapter_up, 'req', axis=0, tiled=True)]
    all_to_all x0 -> x1, waiting for transfers between devices: none -> 102 us  [body(): lax.all_to_all(jnp.stack([adapter_down] * lax.axis_size('req')), 'req', 0...]
    all_to_all x0 -> x1, starting transfers between devices: none -> 21.2 us  [body(): lax.all_to_all(jnp.stack([adapter_down] * lax.axis_size('req')), 'req', 0...]
  transfers between devices with their start and end apart: 3 -> 3, of which waited for: 3 -> 3; matrix products, arithmetic and copies ran while one was open for 3% -> 4% of each run, Pallas kernels for 0% -> 0%
where the time goes in v1:
time: 227 us; the launch traced here: 226 us
  waiting for transfers between devices  173 us (76%)
  starting transfers between devices  21.2 us (9%)
  between operations  13.5 us (6%)
  local copies, waits for them, and re-layouts  9.94 us (4%)
  matrix products  6.65 us (3%)
    all_to_all x1, waiting for transfers between devices, body(): lax.all_to_all(jnp.stack([adapter_down] * lax.axis_size('req')), 'req', 0...  102 us
    all_gather x1, waiting for transfers between devices, body(): lax.all_gather(adapter_up, 'req', axis=0, tiled=True)  36.4 us
    reduce_scatter x1, waiting for transfers between devices, body(): lax.psum_scatter(partial_rows, 'tp', scatter_dimension=1, tiled=True)  33.8 us
    all_to_all x1, starting transfers between devices, body(): lax.all_to_all(jnp.stack([adapter_down] * lax.axis_size('req')), 'req', 0...  21.2 us
  transfers between devices with their start and end apart: 3, of which 3 were waited for; matrix products, arithmetic and copies ran while one was open for 4% of the time, Pallas kernels for 0%

profile of v1, /device:TPU:1, one launch (start us, length us, event | category | flops | bytes accessed | tf_op | source)
XLA Modules:
  0.0 226.4 jit_solution(15551247581610302231)
XLA Ops:
  6.5 0.7 all-gather.2.cloned.1.call-update
  7.3 2.3 %stack.2 = bf16[128,1,512,16]{2,3,1,0:T(8,128)(2,1)} broadcast(bf16[512,16]{0,1:T(8,128)(2,1)} %bitcast.68), dimensions={2,3} | broadcast | bytes 2113536 | tf_op jit(solution)/shard_map/stack | solution.py:60
  9.5 0.0 copy-start.2
  9.6 0.0 copy-start.3
  9.6 21.2 %all-to-all-start = ((bf16[128,1,512,16]{2,3,1,0:T(8,128)(2,1)}), bf16[128,1,512,16]{2,3,1,0:T(8,128)(2,1)}, u32[]{:S(2)}, u32[]{:S(2)}) async-start(bf16[128,1,512,16]{2,3,1,0:T(8,128)(2,1)} %stack.2), calls=%async_computation | async-start | bytes 4194304 | tf_op jit(solution)/shard_map/all_to_all | solution.py:60
  30.7 0.0 reduce-scatter.2.cloned.1.call-start
  30.8 0.8 copy.37
  31.7 0.6 gather_fusion
  32.3 0.2 reduce-window.8
  32.5 0.1 convert_reduce_fusion
  32.6 0.1 fusion.11
  32.7 0.6 fusion.26
  33.3 1.3 fusion.4
  34.6 1.4 convolution_convert_fusion
  36.1 101.9 %all-to-all-done = bf16[128,1,512,16]{2,3,1,0:T(8,128)(2,1)} async-done(((bf16[128,1,512,16]{2,3,1,0:T(8,128)(2,1)}), bf16[128,1,512,16]{2,3,1,0:T(8,128)(2,1)}, u32[]{:S(2)}, u32[]{:S(2)}) %all-to-all-start) | async-done | bytes 2097184 | tf_op jit(solution)/shard_map/all_to_all | solution.py:60
  138.0 2.2 gather_fusion.1
  140.2 0.2 fusion.6
  140.4 36.4 %all-gather.2.cloned.1.call-done = bf16[128,16,2048]{2,1,0:T(8,128)(2,1)} async-done(((bf16[1,16,2048]{2,1,0:T(8,128)(2,1)}), bf16[128,16,2048]{2,1,0:T(8,128)(2,1)}) %all-gather.2.cloned.1.call-update) | async-done | bytes 8388624 | tf_op jit(solution)/shard_map/all_gather | solution.py:62
  176.8 3.9 %gather_fusion.2 = bf16[4,16,2048]{2,1,0:T(8,128)(2,1)S(1)} fusion(bf16[128,16,2048]{2,1,0:T(8,128)(2,1)} %all-gather.2.cloned.1.call-done, s32[1024]{0:T(1024)S(1)} %pad_clamp_fusion), kind=kCustom, calls=%fused_computation.2 | custom fusion | bytes 524304 | tf_op jit(solution)/shard_map/gather | solution.py:66
  180.7 1.0 convolution_bitcast_fusion
  181.8 2.1 convolution_add_fusion
  183.9 0.0 reduce-scatter.2.cloned.1.call-update
  183.9 33.8 %reduce-scatter.2.cloned.1.call-done = f32[256,512]{1,0:T(8,128)} async-done(((f32[256,2048]{1,0:T(8,128)}), f32[256,512]{1,0:T(8,128)}) %reduce-scatter.2.cloned.1.call-update) | async-done | bytes 524304 | tf_op jit(solution)/shard_map/reduce_scatter | solution.py:73
  217.7 1.8 convert_element_type.32
  (18 shorter events, 0.1 us)
Async XLA Ops:
  6.5 175.2 %copy-start = (bf16[512,2048]{1,0:T(8,128)(2,1)S(1)}, bf16[512,2048]{1,0:T(8,128)(2,1)}, u32[]{:S(2)}) copy-start(bf16[512,2048]{1,0:T(8,128)(2,1)} %param.17) | copy-start | bytes 6291460
  6.5 170.2 %all-gather.2.cloned.1.call-start = ((), (), s32[]{:S(2)}) async-start(), calls=%async_computation.2 | async-start | bytes 8454144 | tf_op jit(solution)/shard_map/all_gather | solution.py:62
  9.5 21.2 %copy-start.4 = (bf16[256,512]{1,0:T(8,128)(2,1)S(1)}, bf16[256,512]{1,0:T(8,128)(2,1)}, u32[]{:S(2)}) copy-start(bf16[256,512]{1,0:T(8,128)(2,1)} %param.11) | copy-start | bytes 786436
  9.5 22.1 %copy-start.5 = (s32[1,4]{1,0:T(1,128)S(1)}, s32[1,4]{1,0:T(1,128)}, u32[]{:S(2)}) copy-start(s32[1,4]{1,0:T(1,128)} %param.13) | copy-start | bytes 52
  9.5 22.1 %copy-start.1 = (s32[128]{0:T(128)S(1)}, s32[128]{0:T(128)}, u32[]{:S(2)}) copy-start(s32[128]{0:T(128)} %param.14) | copy-start | bytes 1540
  9.5 22.8 %copy-start.6 = (s32[1,4]{1,0:T(1,128)S(1)}, s32[1,4]{1,0:T(1,128)}, u32[]{:S(2)}) copy-start(s32[1,4]{1,0:T(1,128)} %param.12) | copy-start | bytes 52
  9.5 23.1 %copy-start.2 = (bf16[256,512]{1,0:T(8,128)(2,1)S(1)}, bf16[256,512]{1,0:T(8,128)(2,1)}, u32[]{:S(2)}) copy-start(bf16[256,512]{1,0:T(8,128)(2,1)} %param.10) | copy-start | bytes 786436
  9.6 23.1 %copy-start.3 = (bf16[256,512]{1,0:T(8,128)(2,1)S(1)}, bf16[256,512]{1,0:T(8,128)(2,1)}, u32[]{:S(2)}) copy-start(bf16[256,512]{1,0:T(8,128)(2,1)} %param.9) | copy-start | bytes 786436
  9.6 128.4 %all-to-all-start = ((bf16[128,1,512,16]{2,3,1,0:T(8,128)(2,1)}), bf16[128,1,512,16]{2,3,1,0:T(8,128)(2,1)}, u32[]{:S(2)}, u32[]{:S(2)}) async-start(bf16[128,1,512,16]{2,3,1,0:T(8,128)(2,1)} %stack.2), calls=%async_computation | async-start | bytes 4194304 | tf_op jit(solution)/shard_map/all_to_all | solution.py:60
  30.7 187.0 %reduce-scatter.2.cloned.1.call-start = ((), (), s32[]{:S(2)}) async-start(), calls=%async_computation.3 | async-start | bytes 2621440 | tf_op jit(solution)/shard_map/reduce_scatter | solution.py:73
Sparse Core Ops, SparseCore 0:
  10.5 166.2 all-gather.1
  184.0 33.6 reduce-scatter.1
